TPU v7x, 256 devices: a whole 4x4x8 slice. The times are simulated.
256 devices in a mesh: row: 16 (over y, x), col: 16 (over z, core).
Axes of the slice: x: 4, y: 4, z: 8, core: 2. Of those that a mesh axis runs over, the one named last changes fastest.
Arguments:
- trail_grad: float32 [16384, 16384], P('row', 'col'), may hold values from -20 to 20, as said below
- factor_rows: float32 [16384, 768], P('col', 'row'), may hold values from -0.046875 to 0.046875
- factor_top: float32 [768, 768], replicated, may hold values from -1 to 2, as said below
- rows_grad: float32 [16384, 768], P(('row', 'col')), may hold values from -6 to 6
- top_grad: float32 [768, 768], replicated, may hold values from -6 to 6, as said below
Outputs:
- rows_adjoint: float32 [16384, 768], P(('row', 'col'))
- top_adjoint: float32 [768, 768], replicated
Inputs may be any that keep to these rules, and one draw needn't show every extreme that they name: trail_grad is symmetric once both of its orders are reverted. factor_top is lower triangular with its diagonal between 1 and 2. top_grad is lower triangular.
All inputs are finite; a program needn't handle non-finite values.
Results may differ from a plain program's by a relative error of at most 0.0001.
Values sent between devices are 32-bit elements; how exact they have to be, the bound alone decides.
A program may use at most 64 MiB of HBM per device.

v0:
```python
import jax
import jax.numpy as jnp
from jax import lax
from jax.sharding import PartitionSpec as P

NB = 256
NP = 3
CB = 128
exact_dots = lax.Precision.HIGHEST


def product(left, right):
    return jnp.dot(left, right, precision=exact_dots, preferred_element_type=jnp.float32)


def column_products(left, right):
    return jnp.einsum(
        "ia,ib->ab", left, right, precision=exact_dots, preferred_element_type=jnp.float32
    )


def halve_diagonal(matrix):
    order = matrix.shape[0]
    row_ids = lax.broadcasted_iota(jnp.int32, (order, order), 0)
    col_ids = lax.broadcasted_iota(jnp.int32, (order, order), 1)
    return jnp.where(row_ids > col_ids, matrix, jnp.where(row_ids == col_ids, 0.5 * matrix, 0.0))


def cholesky_adjoint(factor, inverse, gradient):
    inner = halve_diagonal(product(factor.T, gradient))
    middle = product(product(inverse.T, inner), inverse)
    return halve_diagonal(middle + middle.T)


def per_device(trail_grad, factor_rows, factor_top, rows_grad, top_grad):
    row_owner = lax.axis_index("row")
    col_owner = lax.axis_index("col")
    row_owners = lax.axis_size("row")
    col_owners = lax.axis_size("col")
    owned_rows = trail_grad.shape[0]
    tiles_row = owned_rows // CB
    tiles_col = trail_grad.shape[1] // CB
    panel_width = NP * NB
    piece_rows = rows_grad.shape[0]
    panels = lax.all_gather(factor_rows, "row", axis=1, tiled=True)
    global_rows = (
        lax.broadcasted_iota(jnp.int32, (tiles_row, tiles_col), 0) * row_owners + row_owner
    )
    global_cols = (
        lax.broadcasted_iota(jnp.int32, (tiles_row, tiles_col), 1) * col_owners + col_owner
    )
    intersection = (global_rows == global_cols).astype(jnp.float32)
    aligned_rows = jnp.einsum(
        "kq,qtw->ktw",
        intersection,
        panels.reshape(tiles_col, CB, panel_width),
        precision=exact_dots,
        preferred_element_type=jnp.float32,
    ).reshape(owned_rows, panel_width)
    cross_factor = lax.psum_scatter(aligned_rows, "col", scatter_dimension=0, tiled=True)
    row_index = lax.broadcasted_iota(jnp.int32, (panel_width, NB), 0)
    identity = jnp.eye(NB, dtype=jnp.float32)
    adj_here = jnp.zeros((piece_rows, panel_width), jnp.float32)
    adj_top = jnp.zeros((panel_width, panel_width), jnp.float32)
    cross_adjoints = [None] * NP
    for which_panel in reversed(range(NP)):
        col_start = which_panel * NB
        col_end = col_start + NB
        below_diag = jnp.where(row_index >= col_end, factor_top[:, col_start:col_end], 0.0)
        diag_block = factor_top[col_start:col_end, col_start:col_end]
        inverse = jax.scipy.linalg.solve_triangular(diag_block, identity, lower=True)
        partial_rows = product(trail_grad, panels[:, col_start:col_end])
        summed_rows = lax.psum_scatter(partial_rows, "col", scatter_dimension=0, tiled=True)
        rows_cbar = (
            rows_grad[:, col_start:col_end] - 2.0 * summed_rows - product(adj_here, below_diag)
        )
        later_blocks = []
        if which_panel < NP - 1:
            cross_terms = jnp.stack(
                [
                    column_products(cross_adjoints[later_panel], cross_factor[:, col_start:col_end])
                    for later_panel in range(which_panel + 1, NP)
                ]
            )
            cross_summed = lax.psum(cross_terms, ("row", "col"))
            later_blocks = [
                cross_summed[later_panel - which_panel - 1]
                for later_panel in range(which_panel + 1, NP)
            ]
        if later_blocks:
            cross_part = jnp.concatenate([jnp.zeros((col_end, NB), jnp.float32)] + later_blocks, 0)
        else:
            cross_part = jnp.zeros((panel_width, NB), jnp.float32)
        top_masked = jnp.where(row_index >= col_end, top_grad[:, col_start:col_end], 0.0)
        top_cbar = top_masked - (product(adj_top + adj_top.T, below_diag) + cross_part)
        rows_adj = product(rows_cbar, inverse)
        top_adj = product(top_cbar, inverse)
        diag_sum = lax.psum(
            column_products(rows_adj, cross_factor[:, col_start:col_end]), ("row", "col")
        )
        diag_grad = jnp.tril(
            top_grad[col_start:col_end, col_start:col_end]
            - product(top_adj.T, below_diag)
            - diag_sum
        )
        diag_adjoint = cholesky_adjoint(diag_block, inverse, diag_grad)
        cross_adjoints[which_panel] = rows_adj
        adj_here = adj_here.at[:, col_start:col_end].set(rows_adj)
        adj_top = adj_top.at[:, col_start:col_end].set(
            top_adj.at[col_start:col_end].set(diag_adjoint)
        )
    return (adj_here, adj_top)


def solution(mesh):
    placed = (P("row", "col"), P("col", "row"), P(), P(("row", "col"), None), P())
    return jax.shard_map(
        per_device,
        mesh=mesh,
        in_specs=placed,
        out_specs=(P(("row", "col"), None), P()),
        check_vma=False,
    )
```

profile of v0, /device:TPU:97, one launch (start us, length us, event | category | flops | bytes accessed | tf_op | source)
XLA Modules:
  0.0 638.5 jit_solution(12279739426921874140)
XLA Ops:
  7.9 56.5 %all-gather.2.cloned.1.call-done = f32[1024,768]{0,1:T(8,128)} async-done(((f32[1024,48]{0,1:T(8,128)}), f32[1024,768]{0,1:T(8,128)}) %all-gather.2.cloned.1.call-update) | async-done | bytes 3145744 | tf_op jit(solution)/shard_map/all_gather | solution.py:45
  64.5 7.1 %fusion.16 = f32[1024,256]{1,0:T(8,128)} fusion(f32[1024,1024]{1,0:T(8,128)} %param.25, f32[1024,768]{0,1:T(8,128)} %all-gather.2.cloned.1.call-done), kind=kOutput, calls=%fused_computation.40 | convolution fusion | flops 3221225472 | bytes 6291456 | tf_op jit(solution)/shard_map/dot_general | solution.py:13
  71.6 6.6 %fusion.14 = f32[1024,256]{1,0:T(8,128)} fusion(f32[1024,1024]{1,0:T(8,128)} %param.25, f32[1024,768]{0,1:T(8,128)S(1)} %copy-done.2), kind=kOutput, calls=%fused_computation.38 | convolution fusion | flops 3221225472 | bytes 6291456 | tf_op jit(solution)/shard_map/dot_general | solution.py:13
  78.3 6.6 %fusion.12 = f32[1024,256]{1,0:T(8,128)} fusion(f32[1024,1024]{1,0:T(8,128)} %param.25, f32[1024,768]{0,1:T(8,128)S(1)} %copy-done.2), kind=kOutput, calls=%fused_computation.36 | convolution fusion | flops 3221225472 | bytes 6291456 | tf_op jit(solution)/shard_map/dot_general | solution.py:13
  85.2 2.4 copy.50
  87.6 3.3 fusion
  90.9 2.6 copy.52
  93.6 1.6 copy-done
  95.4 3.8 while.15
  96.0 1.3 bitcast_dynamic-update-slice_fusion.6
  97.9 1.3 bitcast_dynamic-update-slice_fusion.6
  99.1 19.7 %custom-call.5 = f32[2,128,128]{1,2,0:T(8,128)S(1)} custom-call(f32[2,128,128]{2,1,0:T(8,128)S(1)} %get-tuple-element.131), custom_call_target="InvertDiagBlocksLowerTriangular" | custom-call | tf_op jit(solution)/shard_map/jit(_solve_triangular)/triangular_solve | solution.py:71
  118.8 3.8 while.16
  119.5 1.3 bitcast_dynamic-update-slice_fusion.7
  121.4 1.3 bitcast_dynamic-update-slice_fusion.7
  122.7 20.3 %custom-call.6 = f32[2,128,128]{1,2,0:T(8,128)} custom-call(f32[2,128,128]{2,1,0:T(8,128)S(1)} %get-tuple-element.132), custom_call_target="InvertDiagBlocksLowerTriangular" | custom-call | tf_op jit(solution)/shard_map/jit(_solve_triangular)/triangular_solve | solution.py:71
  143.0 3.7 while.17
  143.6 1.2 bitcast_dynamic-update-slice_fusion.8
  145.5 1.2 bitcast_dynamic-update-slice_fusion.8
  146.7 20.3 %custom-call.7 = f32[2,128,128]{1,2,0:T(8,128)} custom-call(f32[2,128,128]{2,1,0:T(8,128)S(1)} %get-tuple-element.133), custom_call_target="InvertDiagBlocksLowerTriangular" | custom-call | tf_op jit(solution)/shard_map/jit(_solve_triangular)/triangular_solve | solution.py:71
  169.6 1.2 fusion.80
  171.9 1.2 fusion.91
  174.1 1.6 convolution_subtract_fusion.8
  175.9 13.4 %reduce-scatter.7.cloned.1.call-done = f32[64,256]{1,0:T(8,128)} async-done(((f32[1024,256]{1,0:T(8,128)}), f32[64,256]{1,0:T(8,128)}) %reduce-scatter.7.cloned.1.call-update) | async-done | bytes 65552 | tf_op jit(solution)/shard_map/reduce_scatter | solution.py:73
  189.3 1.5 convolution_subtract_fusion.7
  191.7 56.6 %reduce-scatter.9.cloned.1.call-done = f32[64,256]{1,0:T(8,128)} async-done(((f32[1024,256]{1,0:T(8,128)}), f32[64,256]{1,0:T(8,128)}) %reduce-scatter.9.cloned.1.call-update) | async-done | bytes 65552 | tf_op jit(solution)/shard_map/reduce_scatter | solution.py:73
  248.3 1.5 convolution_subtract_fusion.6
  250.7 60.2 %reduce-scatter.11.cloned.1.call-done = f32[64,768]{1,0:T(8,128)} async-done(((f32[1024,768]{1,0:T(8,128)}), f32[64,768]{1,0:T(8,128)}) %reduce-scatter.11.cloned.1.call-update) | async-done | bytes 196624 | tf_op jit(solution)/shard_map/reduce_scatter | solution.py:60
  310.9 1.3 convolution_bitcast_fusion.3
  312.2 1.3 convolution_bitcast_fusion.4
  314.3 1.9 fusion.85
  316.2 2.0 fusion.96
  320.6 2.0 fusion.22
  322.6 261.0 %all-reduce.6.cloned.1.call-done = (f32[256,256]{1,0:T(8,128)}, f32[256,256]{1,0:T(8,128)}, f32[256,256]{1,0:T(8,128)}, f32[2,256,256]{2,1,0:T(8,128)}, f32[256,256]{1,0:T(8,128)}) async-done(((f32[256,256]{1,0:T(8,128)}, f32[256,256]{1,0:T(8,128)}, f32[256,256]{1,0:T(8,128)}, f32[2,256,256]{2,1,0:T(8,128)}, f32[256,256]{1,0:T(8,128)}), (f32[256,256]{1,0:T(8,128)}, f32[256,256]{1,0:T(8,128)}, ...) | async-done | bytes 1572880 | tf_op jit(solution)/shard_map/psum | solution.py:98
  583.7 2.6 fusion.9
  588.1 1.1 copy.55
  589.3 1.5 pad_bitcast_fusion
  590.9 1.6 copy-done.1
  592.5 3.5 fusion.5
  596.8 2.5 fusion.10
  603.7 1.6 broadcast_select_fusion
  605.3 1.4 copy.58
  606.7 2.0 copy.59
  609.8 6.2 fusion.4
  617.9 2.8 fusion.11
  620.8 1.6 convolution_bitcast_fusion
  624.1 1.8 copy.61
  629.5 2.0 copy.64
  (108 shorter events, 30.1 us)
Async XLA Ops:
  7.2 57.3 %all-gather.2.cloned.1.call-start = ((), (), s32[]{:S(2)}) async-start(), calls=%async_computation.4 | async-start | bytes 3342336 | tf_op jit(solution)/shard_map/all_gather | solution.py:45
  7.9 166.2 %reduce-scatter.5.cloned.1.call-start = ((), (), s32[]{:S(2)}) async-start(), calls=%async_computation.5 | async-start | bytes 1114112 | tf_op jit(solution)/shard_map/reduce_scatter | solution.py:73
  64.5 7.1 %copy-start.2 = (f32[1024,768]{0,1:T(8,128)S(1)}, f32[1024,768]{0,1:T(8,128)}, u32[]{:S(2)}) copy-start(f32[1024,768]{0,1:T(8,128)} %all-gather.2.cloned.1.call-done) | copy-start | bytes 9437188
  71.6 117.7 %reduce-scatter.7.cloned.1.call-start = ((), (), s32[]{:S(2)}) async-start(), calls=%async_computation.6 | async-start | bytes 1114112 | tf_op jit(solution)/shard_map/reduce_scatter | solution.py:73
  78.3 170.0 %reduce-scatter.9.cloned.1.call-start = ((), (), s32[]{:S(2)}) async-start(), calls=%async_computation.7 | async-start | bytes 1114112 | tf_op jit(solution)/shard_map/reduce_scatter | solution.py:73
  85.0 225.9 %reduce-scatter.11.cloned.1.call-start = ((), (), s32[]{:S(2)}) async-start(), calls=%async_computation.8 | async-start | bytes 3342336 | tf_op jit(solution)/shard_map/reduce_scatter | solution.py:60
  93.5 1.7 copy-start
  93.6 490.1 %all-reduce.6.cloned.1.call-start = ((), (), s32[]{:S(2)}) async-start(), calls=%async_computation.9 | async-start | bytes 3145728 | tf_op jit(solution)/shard_map/psum | solution.py:98
  122.7 46.0 %copy-start.11 = (f32[256,256]{1,0:T(8,128)}, f32[256,256]{1,0:T(8,128)S(1)}, u32[]{:S(2)}) copy-start(f32[256,256]{1,0:T(8,128)S(1)} %get-tuple-element.347) | copy-start | bytes 786436
  167.0 6.1 copy-start.16
  169.6 21.2 %copy-start.8 = (f32[128,256]{1,0:T(8,128)}, f32[128,256]{1,0:T(8,128)S(1)}, u32[]{:S(2)}) copy-start(f32[128,256]{1,0:T(8,128)S(1)} %fusion.93) | copy-start | bytes 393220
  173.1 76.7 %copy-start.6 = (f32[128,256]{1,0:T(8,128)}, f32[128,256]{1,0:T(8,128)S(1)}, u32[]{:S(2)}) copy-start(f32[128,256]{1,0:T(8,128)S(1)} %fusion.91) | copy-start | bytes 393220
  174.0 76.7 %copy-start.4 = (f32[128,256]{1,0:T(8,128)}, f32[128,256]{1,0:T(8,128)S(1)}, u32[]{:S(2)}) copy-start(f32[128,256]{1,0:T(8,128)S(1)} %fusion.89) | copy-start | bytes 393220
  250.7 69.8 %copy-start.12 = (f32[64,768]{1,0:T(8,128)}, f32[64,768]{1,0:T(8,128)S(1)}, u32[]{:S(2)}) copy-start(f32[64,768]{1,0:T(8,128)S(1)} %get-tuple-element.184) | copy-start | bytes 589828
  310.9 7.3 %copy-start.13 = (f32[64,768]{1,0:T(8,128)S(1)}, f32[64,768]{1,0:T(8,128)}, u32[]{:S(2)}) copy-start(f32[64,768]{1,0:T(8,128)} %reduce-scatter.11.cloned.1.call-done) | copy-start | bytes 589828
  583.7 3.2 copy-start.9
  589.3 1.5 copy-start.3
  589.3 1.6 copy-start.15
  590.8 1.7 copy-start.1
  592.5 3.5 copy-start.7
  592.5 4.3 copy-start.14
  609.8 6.2 copy-start.5
  620.8 7.0 %copy-start.10 = (f32[768,256]{0,1:T(8,128)S(1)}, f32[768,256]{0,1:T(8,128)}, u32[]{:S(2)}) copy-start(f32[768,256]{0,1:T(8,128)} %copy.62) | copy-start | bytes 2359300
Sparse Core Ops, SparseCore 0:
  10.4 54.0 all-gather.1
  71.7 58.0 reduce-scatter.4
  132.3 56.9 reduce-scatter.6
  191.7 56.5 reduce-scatter.8
  250.7 60.1 reduce-scatter.10
  320.6 263.0 all-reduce.5
where the time goes:
time: 648 us; the launch traced here: 638 us
  waiting for transfers between devices  449 us (69%)
  matrix products  72.5 us (11%)
  other arithmetic  67.5 us (10%)
  local copies, waits for them, and re-layouts  34.5 us (5%)
  between operations  14.9 us (2%)
    psum x1, waiting for transfers between devices, per_device(): lax.psum(column_products(rows_adj, cross_factor[:, col_start:col_end]), (...  261 us
    reduce_scatter x3, waiting for transfers between devices, per_device(): lax.psum_scatter(partial_rows, 'col', scatter_dimension=0, tiled=True)  70 us
    another operation x5, other arithmetic, per_device(): jax.scipy.linalg.solve_triangular(diag_block, identity, lower=True)  60.3 us
    reduce_scatter x1, waiting for transfers between devices, per_device(): lax.psum_scatter(aligned_rows, 'col', scatter_dimension=0, tiled=True)  60.2 us
    all_gather x1, waiting for transfers between devices, per_device(): panels = lax.all_gather(factor_rows, 'row', axis=1, tiled=True)  56.5 us
    dot_general x26, matrix products, product(): jnp.dot(left, right, precision=exact_dots, preferred_element_type=jnp.flo...  55.2 us
  transfers between devices with their start and end apart: 6, of which 5 were waited for; matrix products, arithmetic and copies ran while one was open for 17% of the time, Pallas kernels for 0%

commit v1 on v0

--- a/solution.py
+++ b/solution.py
@@ -96,7 +96,7 @@
         rows_adj = product(rows_cbar, inverse)
         top_adj = product(top_cbar, inverse)
         diag_sum = lax.psum(
-            column_products(rows_adj, cross_factor[:, col_start:col_end]), ("row", "col")
+            lax.psum(column_products(rows_adj, cross_factor[:, col_start:col_end]), "row"), "col"
         )
         diag_grad = jnp.tril(
             top_grad[col_start:col_end, col_start:col_end]

time: 648 us -> 854 us (1.32)
  waiting for transfers between devices: 449 us -> 649 us
    psum x1 -> x3, waiting for transfers between devices: 261 us -> 462 us  [the longest x1 263 us: per_device(): cross_summed = lax.psum(cross_terms, ('row', 'col'))]
  transfers between devices with their start and end apart: 6 -> 8, of which waited for: 5 -> 7; matrix products, arithmetic and copies ran while one was open for 17% -> 14% of each run, Pallas kernels for 0% -> 0%
where the time goes in v1:
time: 854 us; the launch traced here: 843 us
  waiting for transfers between devices  649 us (76%)
  matrix products  74.1 us (9%)
  other arithmetic  67.4 us (8%)
  local copies, waits for them, and re-layouts  36.3 us (4%)
  between operations  15 us (2%)
    psum x1, waiting for transfers between devices, per_device(): cross_summed = lax.psum(cross_terms, ('row', 'col'))  263 us
    psum x1, waiting for transfers between devices, per_device(): lax.psum(lax.psum(column_products(rows_adj, cross_factor[:, col_start:col...  110 us
    psum x1, waiting for transfers between devices, per_device(): lax.psum(column_products(rows_adj, cross_factor[:, col_start:col_end]), '...  88.2 us
    reduce_scatter x3, waiting for transfers between devices, per_device(): lax.psum_scatter(partial_rows, 'col', scatter_dimension=0, tiled=True)  69.4 us
    another operation x5, other arithmetic, per_device(): jax.scipy.linalg.solve_triangular(diag_block, identity, lower=True)  60.3 us
    reduce_scatter x1, waiting for transfers between devices, per_device(): lax.psum_scatter(aligned_rows, 'col', scatter_dimension=0, tiled=True)  60.3 us
    all_gather x1, waiting for transfers between devices, per_device(): panels = lax.all_gather(factor_rows, 'row', axis=1, tiled=True)  56.5 us
    dot_general x26, matrix products, product(): jnp.dot(left, right, precision=exact_dots, preferred_element_type=jnp.flo...  55.2 us
  transfers between devices with their start and end apart: 8, of which 7 were waited for; matrix products, arithmetic and copies ran while one was open for 14% of the time, Pallas kernels for 0%

profile of v1, /device:TPU:97, one launch (start us, length us, event | category | flops | bytes accessed | tf_op | source)
XLA Modules:
  0.0 842.7 jit_solution(18171401651975525231)
XLA Ops:
  7.9 56.5 %all-gather.2.cloned.1.call-done = f32[1024,768]{0,1:T(8,128)} async-done(((f32[1024,48]{0,1:T(8,128)}), f32[1024,768]{0,1:T(8,128)}) %all-gather.2.cloned.1.call-update) | async-done | bytes 3145744 | tf_op jit(solution)/shard_map/all_gather | solution.py:45
  64.5 7.1 fusion.16
  71.6 6.6 fusion.14
  78.3 6.6 fusion.12
  85.2 2.4 copy.50
  87.6 3.3 fusion
  90.9 2.6 copy.52
  93.6 1.6 copy-done
  95.4 4.1 while.15
  96.0 1.4 bitcast_dynamic-update-slice_fusion.6
  98.1 1.4 bitcast_dynamic-update-slice_fusion.6
  99.5 19.7 %custom-call.5 = f32[2,128,128]{1,2,0:T(8,128)S(1)} custom-call(f32[2,128,128]{2,1,0:T(8,128)S(1)} %get-tuple-element.131), custom_call_target="InvertDiagBlocksLowerTriangular" | custom-call | tf_op jit(solution)/shard_map/jit(_solve_triangular)/triangular_solve | solution.py:71
  119.2 4.0 while.16
  119.8 1.4 bitcast_dynamic-update-slice_fusion.7
  121.8 1.4 bitcast_dynamic-update-slice_fusion.7
  123.2 20.3 %custom-call.6 = f32[2,128,128]{1,2,0:T(8,128)} custom-call(f32[2,128,128]{2,1,0:T(8,128)S(1)} %get-tuple-element.132), custom_call_target="InvertDiagBlocksLowerTriangular" | custom-call | tf_op jit(solution)/shard_map/jit(_solve_triangular)/triangular_solve | solution.py:71
  143.5 4.0 while.17
  144.1 1.4 bitcast_dynamic-update-slice_fusion.8
  146.1 1.4 bitcast_dynamic-update-slice_fusion.8
  147.5 20.3 %custom-call.7 = f32[2,128,128]{1,2,0:T(8,128)} custom-call(f32[2,128,128]{2,1,0:T(8,128)S(1)} %get-tuple-element.133), custom_call_target="InvertDiagBlocksLowerTriangular" | custom-call | tf_op jit(solution)/shard_map/jit(_solve_triangular)/triangular_solve | solution.py:71
  174.6 1.6 convolution_subtract_fusion.8
  176.4 12.8 %reduce-scatter.7.cloned.1.call-done = f32[64,256]{1,0:T(8,128)} async-done(((f32[1024,256]{1,0:T(8,128)}), f32[64,256]{1,0:T(8,128)}) %reduce-scatter.7.cloned.1.call-update) | async-done | bytes 65552 | tf_op jit(solution)/shard_map/reduce_scatter | solution.py:73
  189.2 1.5 convolution_subtract_fusion.7
  191.7 56.6 %reduce-scatter.9.cloned.1.call-done = f32[64,256]{1,0:T(8,128)} async-done(((f32[1024,256]{1,0:T(8,128)}), f32[64,256]{1,0:T(8,128)}) %reduce-scatter.9.cloned.1.call-update) | async-done | bytes 65552 | tf_op jit(solution)/shard_map/reduce_scatter | solution.py:73
  248.3 1.5 convolution_subtract_fusion.6
  250.8 60.3 %reduce-scatter.11.cloned.1.call-done = f32[64,768]{1,0:T(8,128)} async-done(((f32[1024,768]{1,0:T(8,128)}), f32[64,768]{1,0:T(8,128)}) %reduce-scatter.11.cloned.1.call-update) | async-done | bytes 196624 | tf_op jit(solution)/shard_map/reduce_scatter | solution.py:60
  311.1 2.0 fusion.85
  313.1 2.0 fusion.94
  315.0 2.0 fusion.98
  320.8 2.0 fusion.96
  323.0 88.2 %all-reduce.14.cloned.1.call-done = (f32[256,256]{1,0:T(8,128)}, f32[256,256]{1,0:T(8,128)}, f32[256,256]{1,0:T(8,128)}) async-done(((f32[256,256]{1,0:T(8,128)}, f32[256,256]{1,0:T(8,128)}, f32[256,256]{1,0:T(8,128)}), (f32[256,256]{1,0:T(8,128)}, f32[256,256]{1,0:T(8,128)}, f32[256,256]{1,0:T(8,128)})) %all-reduce.14.cloned.1.call-update) | async-done | bytes 786448 | tf_op jit(solution)/shard_map/psum | solution.py:99
  411.3 2.0 fusion.22
  413.3 263.3 %all-reduce.10.cloned.1.call-done = (f32[256,256]{1,0:T(8,128)}, f32[2,256,256]{2,1,0:T(8,128)}) async-done(((f32[256,256]{1,0:T(8,128)}, f32[2,256,256]{2,1,0:T(8,128)}), (f32[256,256]{1,0:T(8,128)}, f32[2,256,256]{2,1,0:T(8,128)})) %all-reduce.10.cloned.1.call-update) | async-done | bytes 786448 | tf_op jit(solution)/shard_map/psum | solution.py:85
  676.5 1.9 slice_bitcast_fusion.1
  678.4 110.4 %all-reduce.12.cloned.1.call-done = (f32[256,256]{1,0:T(8,128)}, f32[256,256]{1,0:T(8,128)}, f32[256,256]{1,0:T(8,128)}) async-done(((f32[256,256]{1,0:T(8,128)}, f32[256,256]{1,0:T(8,128)}, f32[256,256]{1,0:T(8,128)}), (f32[256,256]{1,0:T(8,128)}, f32[256,256]{1,0:T(8,128)}, f32[256,256]{1,0:T(8,128)})) %all-reduce.12.cloned.1.call-update) | async-done | bytes 786448 | tf_op jit(solution)/shard_map/psum | solution.py:98
  788.8 2.6 fusion.9
  794.4 1.5 pad_bitcast_fusion
  796.0 1.6 copy-done.1
  797.6 3.3 fusion.5
  801.7 2.5 fusion.10
  808.6 1.6 broadcast_select_fusion
  810.3 1.4 copy.58
  811.8 2.1 copy.59
  813.9 6.2 fusion.4
  822.1 2.8 fusion.11
  824.9 1.6 convolution_bitcast_fusion
  828.2 1.8 copy.61
  833.7 2.0 copy.64
  (116 shorter events, 33.5 us)
Async XLA Ops:
  7.2 57.3 %all-gather.2.cloned.1.call-start = ((), (), s32[]{:S(2)}) async-start(), calls=%async_computation.4 | async-start | bytes 3342336 | tf_op jit(solution)/shard_map/all_gather | solution.py:45
  7.9 166.7 %reduce-scatter.5.cloned.1.call-start = ((), (), s32[]{:S(2)}) async-start(), calls=%async_computation.5 | async-start | bytes 1114112 | tf_op jit(solution)/shard_map/reduce_scatter | solution.py:73
  64.5 7.1 copy-start.2
  71.6 117.7 %reduce-scatter.7.cloned.1.call-start = ((), (), s32[]{:S(2)}) async-start(), calls=%async_computation.6 | async-start | bytes 1114112 | tf_op jit(solution)/shard_map/reduce_scatter | solution.py:73
  78.3 170.0 %reduce-scatter.9.cloned.1.call-start = ((), (), s32[]{:S(2)}) async-start(), calls=%async_computation.7 | async-start | bytes 1114112 | tf_op jit(solution)/shard_map/reduce_scatter | solution.py:73
  85.0 226.1 %reduce-scatter.11.cloned.1.call-start = ((), (), s32[]{:S(2)}) async-start(), calls=%async_computation.8 | async-start | bytes 3342336 | tf_op jit(solution)/shard_map/reduce_scatter | solution.py:60
  93.5 1.7 copy-start
  93.6 317.7 %all-reduce.14.cloned.1.call-start = ((), (), s32[]{:S(2)}) async-start(), calls=%async_computation.11 | async-start | bytes 1572864 | tf_op jit(solution)/shard_map/psum | solution.py:99
  123.1 46.1 %copy-start.11 = (f32[256,256]{1,0:T(8,128)}, f32[256,256]{1,0:T(8,128)S(1)}, u32[]{:S(2)}) copy-start(f32[256,256]{1,0:T(8,128)S(1)} %get-tuple-element.356) | copy-start | bytes 786436
  167.8 5.9 copy-start.17
  170.1 20.6 %copy-start.8 = (f32[128,256]{1,0:T(8,128)}, f32[128,256]{1,0:T(8,128)S(1)}, u32[]{:S(2)}) copy-start(f32[128,256]{1,0:T(8,128)S(1)} %fusion.93) | copy-start | bytes 393220
  173.6 76.2 %copy-start.6 = (f32[128,256]{1,0:T(8,128)}, f32[128,256]{1,0:T(8,128)S(1)}, u32[]{:S(2)}) copy-start(f32[128,256]{1,0:T(8,128)S(1)} %fusion.91) | copy-start | bytes 393220
  174.5 76.2 %copy-start.4 = (f32[128,256]{1,0:T(8,128)}, f32[128,256]{1,0:T(8,128)S(1)}, u32[]{:S(2)}) copy-start(f32[128,256]{1,0:T(8,128)S(1)} %fusion.89) | copy-start | bytes 393220
  250.8 72.0 %copy-start.12 = (f32[64,768]{1,0:T(8,128)}, f32[64,768]{1,0:T(8,128)S(1)}, u32[]{:S(2)}) copy-start(f32[64,768]{1,0:T(8,128)S(1)} %get-tuple-element.187) | copy-start | bytes 589828
  317.0 359.5 %all-reduce.10.cloned.1.call-start = ((), (), s32[]{:S(2)}) async-start(), calls=%async_computation.9 | async-start | bytes 1572864 | tf_op jit(solution)/shard_map/psum | solution.py:85
  322.8 466.0 %all-reduce.12.cloned.1.call-start = ((), (), s32[]{:S(2)}) async-start(), calls=%async_computation.10 | async-start | bytes 1572864 | tf_op jit(solution)/shard_map/psum | solution.py:98
  788.8 3.2 copy-start.9
  794.4 1.5 copy-start.3
  794.4 1.6 copy-start.16
  795.9 1.7 copy-start.1
  797.6 3.3 copy-start.7
  797.6 4.1 copy-start.15
  811.7 2.2 copy-start.13
  811.7 2.2 copy-start.14
  813.9 6.2 copy-start.5
  824.9 7.0 copy-start.10
Sparse Core Ops, SparseCore 0:
  10.4 54.0 all-gather.1
  71.7 57.9 reduce-scatter.4
  132.2 56.9 reduce-scatter.6
  191.6 56.6 reduce-scatter.8
  250.7 60.3 reduce-scatter.10
  317.1 94.0 all-reduce.13
  417.5 258.9 all-reduce.9
  679.0 109.7 all-reduce.11
